TPU v7x, 1024 devices: a whole 4x4x32 slice. The times are simulated.
1024 devices in a mesh: ctx: 256 (over y_hi, x, z), tp: 4 (over y_lo, core).
Axes of the slice: x: 4, y: 4 (y_hi: 2, y_lo: 2; y = y_hi * 2 + y_lo), z: 32, core: 2. Of those that a mesh axis runs over, the one named last changes fastest.
Arguments:
- hyena_q: bfloat16 [65536, 4096], P('ctx', 'tp'), may hold values from -6 to 6
- hyena_k: bfloat16 [65536, 4096], P('ctx', 'tp'), may hold values from -6 to 6
- hyena_v: bfloat16 [65536, 4096], P('ctx', 'tp'), may hold values from -6 to 6
- filters: bfloat16 [256, 128], P('tp'), may hold values from -0.5 to 0.5
- direct: bfloat16 [4096], P('tp'), may hold values from -4 to 4
- queries: bfloat16 [65536, 2048], P('ctx', 'tp'), may hold values from -64 to 64
- keys: bfloat16 [65536, 2048], P('ctx', 'tp'), may hold values from -4 to 4
- values: bfloat16 [65536, 2048], P('ctx', 'tp'), may hold values from -6 to 6
- segment_ids: int32 [65536], P('ctx'), may hold values from 0 to 127, never falling along the last dimension, each value on 1 to 1793 neighbouring positions
- out_weight: bfloat16 [2048, 4096], P(None, 'tp'), may hold values from -0.125 to 0.125
Outputs:
- hyena_out: bfloat16 [65536, 4096], P('ctx', 'tp')
- attn_out: bfloat16 [65536, 4096], P('ctx', 'tp')
Inputs may be any that keep to these rules, and one draw needn't show every extreme that they name: `segment_ids`: ids never fall along the sequence; each document holds 1 to 1793 tokens and one holds exactly 1793.
All inputs are finite; a program needn't handle non-finite values.
Results may differ from a plain program's by a relative error of at most 0.006.
Values may be sent and summed in bfloat16 or wider, within the bound.
A program may use at most 64 MiB of HBM per device.

v0:
```python
import jax
import jax.numpy as jnp
from jax import lax
from jax.sharding import PartitionSpec as P

HD = 128
WINDOW = 8


NEG = -1e30


def shifted(value, axis, steps):
    count = lax.axis_size(axis)
    leading, last = (max(0, -steps), min(count, count - steps))
    return lax.ppermute(value, axis, [(source, source + steps) for source in range(leading, last)])


def toeplitz(filters, rows):
    kernel = filters.shape[1]
    span = rows + kernel - 1
    flipped = filters[:, ::-1]
    padded = jnp.concatenate(
        [flipped, jnp.zeros((filters.shape[0], span + 1 - kernel), filters.dtype)], axis=1
    )
    tiled = jnp.tile(padded, (1, rows))[:, : rows * span]
    return tiled.reshape(filters.shape[0], rows, span)


def hyena_part(hyena_q, hyena_k, hyena_v, filters, direct):
    rows, chans = hyena_k.shape
    groups, kernel = filters.shape
    width = chans // groups
    mixed = (hyena_k.astype(jnp.float32) * hyena_v.astype(jnp.float32)).astype(jnp.bfloat16)
    rim = shifted(mixed[rows - (kernel - 1) :], "ctx", 1)
    extended = jnp.concatenate([rim, mixed], axis=0)
    table = toeplitz(filters, kernel)
    pieces = [extended[b * kernel : b * kernel + 2 * kernel - 1] for b in range(rows // kernel)]
    stacked = jnp.stack(pieces).reshape(len(pieces), 2 * kernel - 1, groups, width)
    conv = jnp.einsum("gts,bsgc->btgc", table, stacked, preferred_element_type=jnp.float32).reshape(
        rows, chans
    )
    return (
        hyena_q.astype(jnp.float32)
        * (conv + direct.astype(jnp.float32) * mixed.astype(jnp.float32))
    ).astype(jnp.bfloat16)


def update(state, query_blk, query_seg, pair, key_seg, diagonal):
    summed, highest, total = state
    rows, heads, size = query_blk.shape
    count = pair.shape[1]
    key_blk = pair[0].reshape(count, heads, size)
    value_blk = pair[1].reshape(count, heads, size)
    score = jnp.einsum(
        "qhd,khd->hqk", query_blk, key_blk, preferred_element_type=jnp.float32
    ) / jnp.sqrt(jnp.float32(size))
    allowed = query_seg[:, None] == key_seg[None, :]
    if diagonal:
        allowed = allowed & (jnp.arange(rows)[:, None] >= jnp.arange(count)[None, :])
    score = jnp.where(allowed[None], score, NEG)
    new_high = jnp.maximum(highest, jnp.max(score, axis=-1))
    expo = jnp.exp(score - new_high[..., None])
    fade = jnp.exp(highest - new_high)
    total = total * fade + jnp.sum(expo, axis=-1)
    summed = summed * fade.T[:, :, None] + jnp.einsum(
        "hqk,khd->qhd", expo.astype(jnp.bfloat16), value_blk, preferred_element_type=jnp.float32
    )
    return (summed, new_high, total)


def local(
    hyena_q, hyena_k, hyena_v, filters, direct, queries, keys, values, segment_ids, out_weight
):
    hyena_out = hyena_part(hyena_q, hyena_k, hyena_v, filters, direct)
    rows, feat = queries.shape
    heads = feat // HD
    query_blk = queries.reshape(rows, heads, HD)
    query_seg = segment_ids + 1
    own = jnp.stack([keys, values])
    start_state = (
        jnp.zeros((rows, heads, HD), jnp.float32),
        jnp.full((heads, rows), NEG, jnp.float32),
        jnp.zeros((heads, rows), jnp.float32),
    )
    state = update(start_state, query_blk, query_seg, own, query_seg, True)

    def fold_remote(current, pair, key_seg):
        return update(current, query_blk, query_seg, pair, key_seg, False)

    def step(turn, carry):
        block, block_seg, current = carry
        block, block_seg = shifted((block, block_seg), "ctx", 1)
        return (block, block_seg, fold_remote(current, block, block_seg))

    _, _, state = lax.fori_loop(0, WINDOW - 1, step, (own, query_seg, state))
    summed, highest, total = state
    attn = (summed / total.T[:, :, None]).reshape(rows, feat).astype(jnp.bfloat16)
    projected = jnp.dot(
        lax.all_gather(attn, "tp", axis=1, tiled=True),
        out_weight,
        preferred_element_type=jnp.float32,
    )
    return (hyena_out, projected.astype(jnp.bfloat16))


def solution(mesh):
    placed = (
        P("ctx", "tp"),
        P("ctx", "tp"),
        P("ctx", "tp"),
        P("tp", None),
        P("tp"),
        P("ctx", "tp"),
        P("ctx", "tp"),
        P("ctx", "tp"),
        P("ctx"),
        P(None, "tp"),
    )
    return jax.shard_map(
        local,
        mesh=mesh,
        in_specs=placed,
        out_specs=(P("ctx", "tp"), P("ctx", "tp")),
        check_vma=False,
    )
```

profile of v0, /device:TPU:24, one launch (start us, length us, event | category | flops | bytes accessed | tf_op | source)
XLA Modules:
  0.0 211.1 jit_solution(2388151033026285886)
XLA Ops:
  7.2 0.7 broadcast_add_fusion
  8.0 1.1 copy.26
  9.1 1.1 copy.25
  10.2 1.1 copy.27
  11.5 1.3 fusion.34
  13.0 0.4 fusion.15
  13.4 155.0 %while.18 = (s32[]{:T(128)}, bf16[2,256,512]{1,2,0:T(8,128)(2,1)S(1)}, s32[256]{0:T(256)S(1)}, f32[256,4,128]{2,0,1:T(8,128)S(1)}, f32[4,256]{1,0:T(4,128)S(1)},...) while((s32[]{:T(128)}, bf16[2,256,512]{1,2,0:T(8,128)(2,1)S(1)}, ...), condition=%wide.region_5.6_spmd, body=%wide.region_2.5_spmd.sunk | while | flops 136907776 | bytes 9511085 | solution.py:96
  13.4 4.0 %collective-permute-start = (bf16[2,256,512]{1,2,0:T(8,128)(2,1)S(1)}, bf16[2,256,512]{1,2,0:T(8,128)(2,1)S(1)}, u32[]{:S(2)}, u32[]{:S(2)}) collective-permute-start(bf16[2,256,512]{1,2,0:T(8,128)(2,1)S(1)} %get-tuple-element.156), channel_id=1, source_target_pairs={{0,4},{4,8},{8,12},{12,16},{16,20},{20,24},{24,28},{28,32},{32,36}... | collective-permute-start | bytes 1572872 | tf_op jit(solution)/shard_map/while/body/eval_jaxpr/ppermute | solution.py:16
  17.4 3.8 %collective-permute-start.1 = (s32[256]{0:T(256)S(1)}, s32[256]{0:T(256)S(1)}, u32[]{:S(2)}, u32[]{:S(2)}) collective-permute-start(s32[256]{0:T(256)S(1)} %get-tuple-element.157), channel_id=1, source_target_pairs={{0,4},{4,8},{8,12},{12,16},{16,20},{20,24},{24,28},{28,32},{32,36}... | collective-permute-start | bytes 3080 | tf_op jit(solution)/shard_map/while/body/eval_jaxpr/ppermute | solution.py:16
  21.2 25.9 %collective-permute-done.1 = s32[256]{0:T(256)S(1)} collective-permute-done((s32[256]{0:T(256)S(1)}, s32[256]{0:T(256)S(1)}, u32[]{:S(2)}, u32[]{:S(2)}) %collective-permute-start.1) | collective-permute-done | bytes 1056 | tf_op jit(solution)/shard_map/while/body/eval_jaxpr/ppermute | solution.py:16
  47.9 0.5 fusion.57
  48.5 1.9 collective-permute-start
  50.4 1.9 collective-permute-start.1
  52.4 16.9 %collective-permute-done.1 = s32[256]{0:T(256)S(1)} collective-permute-done((s32[256]{0:T(256)S(1)}, s32[256]{0:T(256)S(1)}, u32[]{:S(2)}, u32[]{:S(2)}) %collective-permute-start.1) | collective-permute-done | bytes 1056 | tf_op jit(solution)/shard_map/while/body/eval_jaxpr/ppermute | solution.py:16
  70.0 0.5 fusion.57
  70.7 1.9 collective-permute-start
  72.6 1.9 collective-permute-start.1
  74.5 16.0 %collective-permute-done.1 = s32[256]{0:T(256)S(1)} collective-permute-done((s32[256]{0:T(256)S(1)}, s32[256]{0:T(256)S(1)}, u32[]{:S(2)}, u32[]{:S(2)}) %collective-permute-start.1) | collective-permute-done | bytes 1056 | tf_op jit(solution)/shard_map/while/body/eval_jaxpr/ppermute | solution.py:16
  90.7 0.4 select_reduce_fusion.2
  91.3 0.5 fusion.57
  91.9 1.9 collective-permute-start
  93.8 1.9 collective-permute-start.1
  95.8 15.1 %collective-permute-done.1 = s32[256]{0:T(256)S(1)} collective-permute-done((s32[256]{0:T(256)S(1)}, s32[256]{0:T(256)S(1)}, u32[]{:S(2)}, u32[]{:S(2)}) %collective-permute-start.1) | collective-permute-done | bytes 1056 | tf_op jit(solution)/shard_map/while/body/eval_jaxpr/ppermute | solution.py:16
  111.6 0.5 fusion.57
  112.2 1.9 collective-permute-start
  114.2 1.9 collective-permute-start.1
  116.1 14.2 %collective-permute-done.1 = s32[256]{0:T(256)S(1)} collective-permute-done((s32[256]{0:T(256)S(1)}, s32[256]{0:T(256)S(1)}, u32[]{:S(2)}, u32[]{:S(2)}) %collective-permute-start.1) | collective-permute-done | bytes 1056 | tf_op jit(solution)/shard_map/while/body/eval_jaxpr/ppermute | solution.py:16
  130.4 0.4 select_reduce_fusion.2
  131.1 0.5 fusion.57
  131.7 1.9 collective-permute-start
  133.6 1.9 collective-permute-start.1
  135.5 13.3 %collective-permute-done.1 = s32[256]{0:T(256)S(1)} collective-permute-done((s32[256]{0:T(256)S(1)}, s32[256]{0:T(256)S(1)}, u32[]{:S(2)}, u32[]{:S(2)}) %collective-permute-start.1) | collective-permute-done | bytes 1056 | tf_op jit(solution)/shard_map/while/body/eval_jaxpr/ppermute | solution.py:16
  149.0 0.4 select_reduce_fusion.2
  149.6 0.5 fusion.57
  150.2 1.9 collective-permute-start
  152.2 1.9 collective-permute-start.1
  154.1 13.0 %collective-permute-done.1 = s32[256]{0:T(256)S(1)} collective-permute-done((s32[256]{0:T(256)S(1)}, s32[256]{0:T(256)S(1)}, u32[]{:S(2)}, u32[]{:S(2)}) %collective-permute-start.1) | collective-permute-done | bytes 1056 | tf_op jit(solution)/shard_map/while/body/eval_jaxpr/ppermute | solution.py:16
  167.9 0.5 fusion.57
  168.7 0.7 divide_convert_fusion
  170.2 2.1 collective-permute-start.2
  172.7 2.6 %copy.43 = bf16[8,8,128,256]{3,1,2,0:T(8,128)(2,1)S(1)} copy(bf16[8,8,128,256]{3,2,1,0:T(8,128)(2,1)S(1)} %bitcast.78) | data formatting | bytes 8388608
  175.3 2.2 %slice.26 = bf16[64,32640]{1,0:T(8,128)(2,1)} slice(bf16[64,32768]{1,0:T(8,128)(2,1)S(1)} %bitcast.79), slice={[0:64], [0:32640]} | slice | bytes 8355840 | tf_op jit(solution)/shard_map/slice | solution.py:26
  177.5 15.9 %reshape.102 = bf16[64,128,255,1]{2,1,0,3:T(8,128)(2,1)} reshape(bf16[64,32640]{1,0:T(8,128)(2,1)} %slice.26) | data formatting | bytes 8355840 | tf_op jit(solution)/shard_map/reshape | solution.py:27
  193.7 0.4 pad_maximum_fusion
  194.1 3.7 %fusion.11 = f32[2,128,64,16]{1,3,0,2:T(8,128)S(1)} fusion(bf16[64,128,255,1]{2,1,0,3:T(8,128)(2,1)} %reshape.102, bf16[1,255,64,16]{1,3,0,2:T(8,128)(2,1)S(1)} %bitcast.82, bf16[1,255,64,16]{1,3,0,2:T(8,128)(2,1)S(1)} %bitcast.81), kind=kOutput, calls=%fused_computation.17 | convolution fusion | flops 134215680 | bytes 6270976 | tf_op jit(solution)/shard_map/gts,bsgc->btgc/dot_general | solution.py:40
  197.8 0.6 copy.24
  198.7 1.0 copy.34
  199.7 4.6 %convolution_convert_fusion = bf16[256,1024]{1,0:T(8,128)(2,1)} fusion(bf16[256,2048]{0,1:T(8,128)(2,1)} %all-gather.2.cloned.1.call-done, bf16[2048,1024]{1,0:T(8,128)(2,1)} %param.21), kind=kOutput, calls=%fused_computation.20 | convolution fusion | flops 1074003968 | bytes 5767168 | tf_op jit(solution)/shard_map/dot_general | solution.py:99
  (101 shorter events, 6.8 us)
Async XLA Ops:
  7.2 5.8 %copy-start = (bf16[256,512]{1,0:T(8,128)(2,1)S(1)}, bf16[256,512]{1,0:T(8,128)(2,1)}, u32[]{:S(2)}) copy-start(bf16[256,512]{1,0:T(8,128)(2,1)} %param.19) | copy-start | bytes 786436
  7.2 192.5 %all-gather.2.cloned.1.call-start = ((), (), s32[]{:S(2)}) async-start(), calls=%async_computation | async-start | bytes 1310720 | tf_op jit(solution)/shard_map/all_gather | solution.py:100
  13.4 156.1 %copy-start.1 = (bf16[256,1024]{1,0:T(8,128)(2,1)S(1)}, bf16[256,1024]{1,0:T(8,128)(2,1)}, u32[]{:S(2)}) copy-start(bf16[256,1024]{1,0:T(8,128)(2,1)} %param.14) | copy-start | bytes 1572868
  13.4 156.3 %copy-start.2 = (bf16[256,1024]{1,0:T(8,128)(2,1)S(1)}, bf16[256,1024]{1,0:T(8,128)(2,1)}, u32[]{:S(2)}) copy-start(bf16[256,1024]{1,0:T(8,128)(2,1)} %param.13) | copy-start | bytes 1572868
  13.4 33.8 %collective-permute-start = (bf16[2,256,512]{1,2,0:T(8,128)(2,1)S(1)}, bf16[2,256,512]{1,2,0:T(8,128)(2,1)S(1)}, u32[]{:S(2)}, u32[]{:S(2)}) collective-permute-start(bf16[2,256,512]{1,2,0:T(8,128)(2,1)S(1)} %get-tuple-element.156), channel_id=1, source_target_pairs={{0,4},{4,8},{8,12},{12,16},{16,20},{20,24},{24,28},{28,32},{32,36}... | collective-permute-start | bytes 1572872 | tf_op jit(solution)/shard_map/while/body/eval_jaxpr/ppermute | solution.py:16
  17.4 29.7 %collective-permute-start.1 = (s32[256]{0:T(256)S(1)}, s32[256]{0:T(256)S(1)}, u32[]{:S(2)}, u32[]{:S(2)}) collective-permute-start(s32[256]{0:T(256)S(1)} %get-tuple-element.157), channel_id=1, source_target_pairs={{0,4},{4,8},{8,12},{12,16},{16,20},{20,24},{24,28},{28,32},{32,36}... | collective-permute-start | bytes 3080 | tf_op jit(solution)/shard_map/while/body/eval_jaxpr/ppermute | solution.py:16
  48.5 20.8 %collective-permute-start = (bf16[2,256,512]{1,2,0:T(8,128)(2,1)S(1)}, bf16[2,256,512]{1,2,0:T(8,128)(2,1)S(1)}, u32[]{:S(2)}, u32[]{:S(2)}) collective-permute-start(bf16[2,256,512]{1,2,0:T(8,128)(2,1)S(1)} %get-tuple-element.156), channel_id=1, source_target_pairs={{0,4},{4,8},{8,12},{12,16},{16,20},{20,24},{24,28},{28,32},{32,36}... | collective-permute-start | bytes 1572872 | tf_op jit(solution)/shard_map/while/body/eval_jaxpr/ppermute | solution.py:16
  50.4 18.8 %collective-permute-start.1 = (s32[256]{0:T(256)S(1)}, s32[256]{0:T(256)S(1)}, u32[]{:S(2)}, u32[]{:S(2)}) collective-permute-start(s32[256]{0:T(256)S(1)} %get-tuple-element.157), channel_id=1, source_target_pairs={{0,4},{4,8},{8,12},{12,16},{16,20},{20,24},{24,28},{28,32},{32,36}... | collective-permute-start | bytes 3080 | tf_op jit(solution)/shard_map/while/body/eval_jaxpr/ppermute | solution.py:16
  70.7 20.0 %collective-permute-start = (bf16[2,256,512]{1,2,0:T(8,128)(2,1)S(1)}, bf16[2,256,512]{1,2,0:T(8,128)(2,1)S(1)}, u32[]{:S(2)}, u32[]{:S(2)}) collective-permute-start(bf16[2,256,512]{1,2,0:T(8,128)(2,1)S(1)} %get-tuple-element.156), channel_id=1, source_target_pairs={{0,4},{4,8},{8,12},{12,16},{16,20},{20,24},{24,28},{28,32},{32,36}... | collective-permute-start | bytes 1572872 | tf_op jit(solution)/shard_map/while/body/eval_jaxpr/ppermute | solution.py:16
  72.6 17.9 %collective-permute-start.1 = (s32[256]{0:T(256)S(1)}, s32[256]{0:T(256)S(1)}, u32[]{:S(2)}, u32[]{:S(2)}) collective-permute-start(s32[256]{0:T(256)S(1)} %get-tuple-element.157), channel_id=1, source_target_pairs={{0,4},{4,8},{8,12},{12,16},{16,20},{20,24},{24,28},{28,32},{32,36}... | collective-permute-start | bytes 3080 | tf_op jit(solution)/shard_map/while/body/eval_jaxpr/ppermute | solution.py:16
  91.9 19.0 %collective-permute-start = (bf16[2,256,512]{1,2,0:T(8,128)(2,1)S(1)}, bf16[2,256,512]{1,2,0:T(8,128)(2,1)S(1)}, u32[]{:S(2)}, u32[]{:S(2)}) collective-permute-start(bf16[2,256,512]{1,2,0:T(8,128)(2,1)S(1)} %get-tuple-element.156), channel_id=1, source_target_pairs={{0,4},{4,8},{8,12},{12,16},{16,20},{20,24},{24,28},{28,32},{32,36}... | collective-permute-start | bytes 1572872 | tf_op jit(solution)/shard_map/while/body/eval_jaxpr/ppermute | solution.py:16
  93.8 17.0 %collective-permute-start.1 = (s32[256]{0:T(256)S(1)}, s32[256]{0:T(256)S(1)}, u32[]{:S(2)}, u32[]{:S(2)}) collective-permute-start(s32[256]{0:T(256)S(1)} %get-tuple-element.157), channel_id=1, source_target_pairs={{0,4},{4,8},{8,12},{12,16},{16,20},{20,24},{24,28},{28,32},{32,36}... | collective-permute-start | bytes 3080 | tf_op jit(solution)/shard_map/while/body/eval_jaxpr/ppermute | solution.py:16
  112.2 18.2 %collective-permute-start = (bf16[2,256,512]{1,2,0:T(8,128)(2,1)S(1)}, bf16[2,256,512]{1,2,0:T(8,128)(2,1)S(1)}, u32[]{:S(2)}, u32[]{:S(2)}) collective-permute-start(bf16[2,256,512]{1,2,0:T(8,128)(2,1)S(1)} %get-tuple-element.156), channel_id=1, source_target_pairs={{0,4},{4,8},{8,12},{12,16},{16,20},{20,24},{24,28},{28,32},{32,36}... | collective-permute-start | bytes 1572872 | tf_op jit(solution)/shard_map/while/body/eval_jaxpr/ppermute | solution.py:16
  114.2 16.1 %collective-permute-start.1 = (s32[256]{0:T(256)S(1)}, s32[256]{0:T(256)S(1)}, u32[]{:S(2)}, u32[]{:S(2)}) collective-permute-start(s32[256]{0:T(256)S(1)} %get-tuple-element.157), channel_id=1, source_target_pairs={{0,4},{4,8},{8,12},{12,16},{16,20},{20,24},{24,28},{28,32},{32,36}... | collective-permute-start | bytes 3080 | tf_op jit(solution)/shard_map/while/body/eval_jaxpr/ppermute | solution.py:16
  131.7 17.3 %collective-permute-start = (bf16[2,256,512]{1,2,0:T(8,128)(2,1)S(1)}, bf16[2,256,512]{1,2,0:T(8,128)(2,1)S(1)}, u32[]{:S(2)}, u32[]{:S(2)}) collective-permute-start(bf16[2,256,512]{1,2,0:T(8,128)(2,1)S(1)} %get-tuple-element.156), channel_id=1, source_target_pairs={{0,4},{4,8},{8,12},{12,16},{16,20},{20,24},{24,28},{28,32},{32,36}... | collective-permute-start | bytes 1572872 | tf_op jit(solution)/shard_map/while/body/eval_jaxpr/ppermute | solution.py:16
  133.6 15.2 %collective-permute-start.1 = (s32[256]{0:T(256)S(1)}, s32[256]{0:T(256)S(1)}, u32[]{:S(2)}, u32[]{:S(2)}) collective-permute-start(s32[256]{0:T(256)S(1)} %get-tuple-element.157), channel_id=1, source_target_pairs={{0,4},{4,8},{8,12},{12,16},{16,20},{20,24},{24,28},{28,32},{32,36}... | collective-permute-start | bytes 3080 | tf_op jit(solution)/shard_map/while/body/eval_jaxpr/ppermute | solution.py:16
  150.2 17.0 %collective-permute-start = (bf16[2,256,512]{1,2,0:T(8,128)(2,1)S(1)}, bf16[2,256,512]{1,2,0:T(8,128)(2,1)S(1)}, u32[]{:S(2)}, u32[]{:S(2)}) collective-permute-start(bf16[2,256,512]{1,2,0:T(8,128)(2,1)S(1)} %get-tuple-element.156), channel_id=1, source_target_pairs={{0,4},{4,8},{8,12},{12,16},{16,20},{20,24},{24,28},{28,32},{32,36}... | collective-permute-start | bytes 1572872 | tf_op jit(solution)/shard_map/while/body/eval_jaxpr/ppermute | solution.py:16
  152.2 14.9 %collective-permute-start.1 = (s32[256]{0:T(256)S(1)}, s32[256]{0:T(256)S(1)}, u32[]{:S(2)}, u32[]{:S(2)}) collective-permute-start(s32[256]{0:T(256)S(1)} %get-tuple-element.157), channel_id=1, source_target_pairs={{0,4},{4,8},{8,12},{12,16},{16,20},{20,24},{24,28},{28,32},{32,36}... | collective-permute-start | bytes 3080 | tf_op jit(solution)/shard_map/while/body/eval_jaxpr/ppermute | solution.py:16
  168.5 3.8 %copy-start.4 = (bf16[64,128]{1,0:T(8,128)(2,1)S(1)}, bf16[64,128]{1,0:T(8,128)(2,1)}, u32[]{:S(2)}) copy-start(bf16[64,128]{1,0:T(8,128)(2,1)} %param.15) | copy-start | bytes 49156
  170.2 23.5 %collective-permute-start.2 = (bf16[127,1024]{0,1:T(8,128)(2,1)S(1)}, bf16[127,1024]{0,1:T(8,128)(2,1)S(1)}, u32[]{:S(2)}, u32[]{:S(2)}) collective-permute-start(bf16[127,1024]{0,1:T(8,128)(2,1)S(1)} %slice.24), channel_id=1, source_target_pairs={{0,4},{4,8},{8,12},{12,16},{16,20},{20,24},{24,28},{28,32},{32,36}... | collective-permute-start | bytes 780296 | tf_op jit(solution)/shard_map/ppermute | solution.py:16
  177.5 15.9 %copy-start.3 = (bf16[256,1024]{1,0:T(8,128)(2,1)S(1)}, bf16[256,1024]{1,0:T(8,128)(2,1)}, u32[]{:S(2)}) copy-start(bf16[256,1024]{1,0:T(8,128)(2,1)} %param.12) | copy-start | bytes 1572868
  177.5 16.1 %copy-start.5 = (bf16[1024]{0:T(1024)(128)(2,1)S(1)}, bf16[1024]{0:T(1024)(128)(2,1)}, u32[]{:S(2)}) copy-start(bf16[1024]{0:T(1024)(128)(2,1)} %param.16) | copy-start | bytes 6148
Sparse Core Ops, SparseCore 0:
  169.6 15.8 all-gather.1
where the time goes:
time: 212 us; the launch traced here: 211 us
  waiting for transfers between devices  114 us (54%)
  starting transfers between devices  33 us (16%)
  local copies, waits for them, and re-layouts  27.6 us (13%)
  matrix products  16.3 us (8%)
  between operations  14.3 us (7%)
  other arithmetic  5.06 us (2%)
    ppermute x15, waiting for transfers between devices, shifted(): lax.ppermute(value, axis, [(source, source + steps) for source in range(l...  114 us
    ppermute x15, starting transfers between devices, shifted(): lax.ppermute(value, axis, [(source, source + steps) for source in range(l...  32.9 us
    reshape x1, local copies, waits for them, and re-layouts, toeplitz(): return tiled.reshape(filters.shape[0], rows, span)  15.9 us
    unnamed x21, local copies, waits for them, and re-layouts  7.48 us
    dot_general x1, matrix products, local(): jnp.dot(lax.all_gather(attn, 'tp', axis=1, tiled=True), out_weight, prefe...  4.59 us
  transfers between devices with their start and end apart: 16, of which 7 were waited for; matrix products, arithmetic and copies ran while one was open for 14% of the time, Pallas kernels for 0%

commit v1 on v0

v1 whole, which is shorter than its diff:
```python
import functools
import math

import jax
import jax.numpy as jnp
from jax import lax
from jax.experimental import pallas as pl
from jax.experimental.pallas import tpu as pltpu
from jax.sharding import PartitionSpec as P

HD = 128
WINDOW = 8
TAPS = 128
GROUP = 16
KEY_HOPS = 2
QUERY_HOPS = WINDOW - 1 - KEY_HOPS
NEG = -1e30
MESH = pl.DeviceIdType.MESH


def plan(heads, blocks):
    chunk, lag = 1.41, 1.9
    free = {"neg": 0.0, "pos": 0.0, "tp": 0.0, "mate": 0.0}
    ready = {}
    order = []
    todo = []

    def add(name, needs, cost, link=None, size=1.0, rank=0):
        todo.append(dict(name=name, needs=needs, cost=cost, link=link, size=size, rank=rank))

    for r in range(1, QUERY_HOPS + 1):
        for h in range(heads):
            add(("q", h, r), [("q", h, r - 1)] if r > 1 else [], 0.03, "neg", 1.0, r)
    for r in range(1, KEY_HOPS + 1):
        for h in range(heads):
            add(("k", h, r), [("k", h, r - 1)] if r > 1 else [], 0.03, "pos", 1.0, r)
        for h in range(heads):
            add(("v", h, r), [("v", h, r - 1)] if r > 1 else [("vt", h)], 0.03, "pos", 1.0, r)
    for h in range(heads):
        add(("vt", h), [], 0.15, rank=1)
        add(("halo", h), [("mix",), ("sent", "v", heads - 1, KEY_HOPS)], 0.03, "pos", 1.0, 5)
    add(("mix",), [], 1.0, rank=2)
    for d in range(KEY_HOPS + 1):
        add(("segk", d), [("q", 0, 1)] if d == 0 else [("k", 0, d)], 0.1, rank=3)
    for h in range(heads):
        for a in range(QUERY_HOPS, 0, -1):
            add(("part", h, a), [("q", h, a), ("k", h, KEY_HOPS), ("v", h, KEY_HOPS), ("segk", KEY_HOPS)], 0.4, rank=10 + (0 if a == QUERY_HOPS else 1))
        for d in range(KEY_HOPS + 1):
            need = [("k", h, d), ("v", h, d)] if d else [("vt", h)]
            add(("local", h, d), need + [("segk", d)] + ([("local", h, d - 1)] if d else []), 0.4, rank=20 + d)
        for a in range(QUERY_HOPS, 0, -1):
            need = [("part", h, a)] + ([("o", h, a + 1)] if a < QUERY_HOPS else [])
            add(("o", h, a), need, 0.2 if a < QUERY_HOPS else 0.05, "pos", 1.0, 4)
        add(("home", h), [("o", h, 1), ("local", h, KEY_HOPS)], 0.3, rank=5)
        add(("g0", h), [("home", h)], 0.03, "mate", 0.1, 6)
        add(("g1", h), [("home", h)], 0.03, "tp", 1.0, 5)
        add(("g2", h), [("g1", h)], 0.03, "mate", 0.1, 5)
    for p in range(heads // 2):
        for j, kind in enumerate(("home", "g0", "g1", "g2")):
            add(("proj", p, j), [(kind, 2 * p), (kind, 2 * p + 1)], 0.4, rank=30 + p * 4 + j)
    add(("taps",), [], 0.5, rank=40)
    for c in range(blocks):
        add(("hyena", c), [("taps",), ("mix",)] + [("halo", h) for h in range(heads)], 1.2, rank=50)

    now = 0.0
    while todo:
        best = None
        horizon = None
        for item in todo:
            when = 0.0
            for need in item["needs"]:
                when = max(when, ready.get(need, math.inf))
            if when <= now:
                if best is None or item["rank"] < best["rank"]:
                    best = item
            elif when < math.inf:
                horizon = when if horizon is None else min(horizon, when)
        if best is None:
            now = horizon
            continue
        todo.remove(best)
        order.append(best["name"])
        now += best["cost"]
        if best["link"]:
            begin = max(now, free[best["link"]])
            free[best["link"]] = begin + best["size"] * chunk
            ready[best["name"]] = free[best["link"]] + lag
            ready[("sent",) + best["name"]] = now
        else:
            ready[best["name"]] = now
    return order


def merge(first, second):
    high_a, total_a, sum_a = first
    high_b, total_b, sum_b = second
    high = jnp.maximum(high_a, high_b)
    fade_a, fade_b = jnp.exp2(high_a - high), jnp.exp2(high_b - high)
    return high, total_a * fade_a + total_b * fade_b, sum_a * fade_a + sum_b * fade_b


def kernel(
    heads,
    order,
    hq_hbm, hk_hbm, hv_hbm, filters_hbm, direct_hbm, q_hbm, k_hbm, v_hbm, seg_hbm, w_hbm,
    hyena_out, attn_out,
    hq, hk, hv, filters, direct, q_own, k_own, v_own, vt_own, seg_own, weight,
    q_in, segq_in, k_in, vt_in, segk_in, segk_col, ext, taps,
    part_sum, part_stat, out_sum, out_stat, in_sum, in_stat, local_sum, local_stat,
    attn, attn_in, total,
    load_sem, head_sem, q_sem, k_sem, v_sem, segq_sem, segk_sem, halo_sem, o_sem, ostat_sem, g_sem,
):
    ctx, tp = lax.axis_index("ctx"), lax.axis_index("tp")
    count = lax.axis_size("ctx")
    right, left = lax.rem(ctx + 1, count), lax.rem(ctx + count - 1, count)
    mate = tp + 1 - 2 * lax.rem(tp, 2)
    across = lax.rem(tp + 2, 4)
    diagonal = lax.rem(mate + 2, 4)
    rows, chans = hk.shape
    scale = math.log2(math.e) / math.sqrt(HD)

    loads = {}

    def load(name, source, target, sem):
        loads[name] = pltpu.make_async_copy(source, target, sem)
        loads[name].start()

    for h in range(heads):
        load(("q", h), q_hbm.at[:, pl.ds(h * HD, HD)], q_own.at[h], head_sem.at[0, h])
        load(("k", h), k_hbm.at[:, pl.ds(h * HD, HD)], k_own.at[h], head_sem.at[1, h])
        load(("v", h), v_hbm.at[:, pl.ds(h * HD, HD)], v_own.at[h], head_sem.at[2, h])
    load("seg", seg_hbm, seg_own, load_sem.at[0])
    load("hk", hk_hbm, hk, load_sem.at[1])
    load("hv", hv_hbm, hv, load_sem.at[2])
    load("filters", filters_hbm, filters, load_sem.at[3])
    load("direct", direct_hbm, direct, load_sem.at[4])
    load("hq", hq_hbm, hq, load_sem.at[5])
    load("weight", w_hbm, weight, load_sem.at[6])

    done = set()

    def loaded(name):
        if name not in done:
            done.add(name)
            loads[name].wait()

    barrier = pltpu.get_barrier_semaphore()
    for peer in ({"ctx": left}, {"ctx": right}, {"tp": mate}, {"tp": across}):
        pl.semaphore_signal(barrier, inc=1, device_id=peer, device_id_type=MESH)
    pl.semaphore_wait(barrier, 4)

    copies = {}

    def copy(name, source, target, sems, index, peer):
        copies[name] = pltpu.make_async_remote_copy(
            src_ref=source,
            dst_ref=target,
            send_sem=sems.at[(0,) + index],
            recv_sem=sems.at[(1,) + index],
            device_id=peer,
            device_id_type=MESH,
        )

    for r in range(1, QUERY_HOPS + 1):
        for h in range(heads):
            copy(("q", h, r), q_own.at[h] if r == 1 else q_in.at[r - 2, h], q_in.at[r - 1, h], q_sem, (r - 1, h), {"ctx": left})
            copy(("o", h, r), out_sum.at[r - 1, h], in_sum.at[r - 1, h], o_sem, (r - 1, h), {"ctx": right})
            copy(("ostat", h, r), out_stat.at[r - 1, h], in_stat.at[r - 1, h], ostat_sem, (r - 1, h), {"ctx": right})
        copy(("segq", r), seg_own if r == 1 else segq_in.at[r - 2], segq_in.at[r - 1], segq_sem, (r - 1,), {"ctx": left})
    for r in range(1, KEY_HOPS + 1):
        for h in range(heads):
            copy(("k", h, r), k_own.at[h] if r == 1 else k_in.at[r - 2, h], k_in.at[r - 1, h], k_sem, (r - 1, h), {"ctx": right})
            copy(("v", h, r), vt_own.at[h] if r == 1 else vt_in.at[r - 2, h], vt_in.at[r - 1, h], v_sem, (r - 1, h), {"ctx": right})
        copy(("segk", r), seg_own if r == 1 else segk_in.at[r - 2], segk_in.at[r - 1], segk_sem, (r - 1,), {"ctx": right})
    strip = chans // heads
    for h in range(heads):
        lanes = pl.ds(h * strip, strip)
        copy(("halo", h), ext.at[pl.ds(rows, TAPS), lanes], ext.at[pl.ds(0, TAPS), lanes], halo_sem, (h,), {"ctx": right})
        half = pl.ds(h % 2 * HD, HD)
        mine = attn.at[h // 2, :, half]
        copy(("g0", h), mine, attn_in.at[0, h // 2, :, half], g_sem, (0, h), {"tp": mate})
        copy(("g1", h), mine, attn_in.at[1, h // 2, :, half], g_sem, (1, h), {"tp": across})
        copy(("g2", h), attn_in.at[1, h // 2, :, half], attn_in.at[2, h // 2, :, half], g_sem, (2, h), {"tp": mate})

    got = set()

    def arrived(name):
        if name not in got:
            got.add(name)
            copies[name].wait_recv()

    def send(name):
        copies[name].start()

    def column(row):
        return jnp.transpose(jnp.broadcast_to(row.astype(jnp.float32), (HD, rows)))

    def partial(query, query_seg, key, value_t, key_col, causal):
        score = lax.dot_general(key[...], query[...], (((1,), (1,)), ((), ())), preferred_element_type=jnp.float32)
        col = key_col[...]
        allowed = jnp.concatenate([col] * (rows // HD), axis=1) == query_seg[...].astype(jnp.float32)
        if causal:
            allowed = allowed & (
                lax.broadcasted_iota(jnp.int32, (rows, rows), 0) <= lax.broadcasted_iota(jnp.int32, (rows, rows), 1)
            )
        score = jnp.where(allowed, score * scale, NEG)
        high = jnp.max(score, axis=0, keepdims=True)
        expo = jnp.exp2(score - high)
        amount = jnp.sum(expo, axis=0, keepdims=True)
        summed = jnp.dot(value_t[...], expo.astype(jnp.bfloat16), preferred_element_type=jnp.float32)
        return high, amount, summed

    def keep(state, stat_ref, sum_ref):
        stat_ref[0:1, :] = state[0]
        stat_ref[1:2, :] = state[1]
        sum_ref[...] = state[2].astype(sum_ref.dtype)

    def fetch(stat_ref, sum_ref):
        return stat_ref[0:1, :], stat_ref[1:2, :], sum_ref[...].astype(jnp.float32)

    def step_q(h, r):
        if r == 1:
            loaded(("q", h))
            if h == 0:
                loaded("seg")
        else:
            arrived(("q", h, r - 1))
            if h == 0:
                arrived(("segq", r - 1))
        if h == 0:
            send(("segq", r))
        send(("q", h, r))

    def step_k(h, r):
        if r == 1:
            loaded(("k", h))
            if h == 0:
                loaded("seg")
        else:
            arrived(("k", h, r - 1))
            if h == 0:
                arrived(("segk", r - 1))
        if h == 0:
            send(("segk", r))
        send(("k", h, r))

    def step_vt(h):
        loaded(("v", h))
        vt_own[h] = jnp.transpose(v_own[h])

    def step_v(h, r):
        if r > 1:
            arrived(("v", h, r - 1))
        send(("v", h, r))

    def step_mix():
        loaded("hk")
        loaded("hv")
        for lo in range(0, rows, 64):
            ext[pl.ds(TAPS + lo, 64), :] = (
                hk[pl.ds(lo, 64), :].astype(jnp.float32) * hv[pl.ds(lo, 64), :].astype(jnp.float32)
            ).astype(jnp.bfloat16)

    def step_halo(h):
        send(("halo", h))

    def step_segk(d):
        if d == 0:
            loaded("seg")
            segk_col[0] = column(seg_own[...])
        else:
            arrived(("segk", d))
            segk_col[d] = column(segk_in[d - 1])

    def step_part(h, a):
        arrived(("q", h, a))
        arrived(("segq", a))
        arrived(("k", h, KEY_HOPS))
        arrived(("v", h, KEY_HOPS))
        state = partial(q_in.at[a - 1, h], segq_in.at[a - 1], k_in.at[KEY_HOPS - 1, h], vt_in.at[KEY_HOPS - 1, h], segk_col.at[KEY_HOPS], False)
        if a == QUERY_HOPS:
            keep(state, out_stat.at[a - 1, h], out_sum.at[a - 1, h])
        else:
            keep(state, part_stat.at[a - 1, h], part_sum.at[a - 1, h])

    def step_local(h, d):
        if d == 0:
            state = partial(q_own.at[h], seg_own, k_own.at[h], vt_own.at[h], segk_col.at[0], True)
        else:
            arrived(("k", h, d))
            arrived(("v", h, d))
            state = partial(q_own.at[h], seg_own, k_in.at[d - 1, h], vt_in.at[d - 1, h], segk_col.at[d], False)
            state = merge(fetch(local_stat.at[h], local_sum.at[h]), state)
        keep(state, local_stat.at[h], local_sum.at[h])

    def step_o(h, a):
        if a < QUERY_HOPS:
            arrived(("o", h, a + 1))
            arrived(("ostat", h, a + 1))
            state = merge(fetch(part_stat.at[a - 1, h], part_sum.at[a - 1, h]), fetch(in_stat.at[a, h], in_sum.at[a, h]))
            keep(state, out_stat.at[a - 1, h], out_sum.at[a - 1, h])
        send(("o", h, a))
        send(("ostat", h, a))

    def step_home(h):
        arrived(("o", h, 1))
        arrived(("ostat", h, 1))
        _, amount, summed = merge(fetch(local_stat.at[h], local_sum.at[h]), fetch(in_stat.at[0, h], in_sum.at[0, h]))
        result = jnp.transpose(summed / amount)
        attn[h // 2, :, pl.ds(h % 2 * HD, HD)] = result.astype(jnp.bfloat16)

    def step_g0(h):
        send(("g0", h))

    def step_g1(h):
        send(("g1", h))

    def step_g2(h):
        arrived(("g1", h))
        send(("g2", h))

    projected = []
    width = 256

    def step_proj(p, j):
        loaded("weight")
        if j:
            for h in (2 * p, 2 * p + 1):
                arrived((("g0", "g1", "g2")[j - 1], h))
        block = attn[p] if j == 0 else attn_in[j - 1, p]
        owner = (tp, mate, across, diagonal)[j]
        start = pl.multiple_of(owner * (heads * HD) + p * 2 * HD, 2 * HD)
        first, last = not projected, len(projected) == 2 * heads - 1
        projected.append((p, j))
        for lo in range(0, chans, width):
            lanes = pl.ds(lo, width)
            term = jnp.dot(block, weight[pl.ds(start, 2 * HD), lanes], preferred_element_type=jnp.float32)
            if not first:
                term = total[:, lanes] + term
            if last:
                attn_out[:, lanes] = term.astype(jnp.bfloat16)
            else:
                total[:, lanes] = term

    def step_taps():
        loaded("filters")
        tap = lax.broadcasted_iota(jnp.int32, (TAPS, 2 * TAPS), 0)
        place = lax.broadcasted_iota(jnp.int32, (TAPS, 2 * TAPS), 1)
        flip = jnp.where(tap + place == TAPS, 1.0, 0.0).astype(jnp.bfloat16)
        taps[...] = jnp.dot(filters[...], flip, preferred_element_type=jnp.float32)

    def step_hyena(c):
        if c == 0:
            for h in range(heads):
                arrived(("halo", h))
            loaded("hq")
            loaded("direct")
        lanes = pl.ds(c * 128, 128)
        before = ext[pl.ds(0, TAPS), lanes]
        before = jnp.where(ctx == 0, jnp.zeros_like(before), before)
        upper, lower = ext[pl.ds(TAPS, TAPS), lanes], ext[pl.ds(2 * TAPS, TAPS), lanes]
        data = jnp.concatenate(
            [jnp.concatenate([before, upper], axis=0), jnp.concatenate([upper, lower], axis=0)], axis=1
        )
        group = lax.rem(lax.broadcasted_iota(jnp.int32, (TAPS, 2 * TAPS), 1), 128) // GROUP
        conv = jnp.zeros((TAPS, 2 * TAPS), jnp.float32)
        per = 128 // GROUP
        for g in range(per):
            row = jnp.broadcast_to(taps[pl.ds(c * per + g, 1), :], (TAPS, 2 * TAPS))
            table = pltpu.roll(row, 0, 1, stride=1, stride_axis=0).astype(jnp.bfloat16)
            conv = jnp.where(group == g, jnp.dot(table, data, preferred_element_type=jnp.float32), conv)
        gain = direct[:, lanes].astype(jnp.float32)
        for b, mixed in enumerate((upper, lower)):
            span = pl.ds(b * TAPS, TAPS)
            hyena_out[span, lanes] = (
                hq[span, lanes].astype(jnp.float32)
                * (conv[:, b * TAPS : (b + 1) * TAPS] + gain * mixed.astype(jnp.float32))
            ).astype(jnp.bfloat16)

    steps = dict(
        q=step_q, k=step_k, vt=step_vt, v=step_v, mix=step_mix, halo=step_halo, segk=step_segk, part=step_part,
        local=step_local, o=step_o, home=step_home, g0=step_g0, g1=step_g1, g2=step_g2, proj=step_proj,
        taps=step_taps, hyena=step_hyena,
    )
    for name in order:
        steps[name[0]](*name[1:])
    for name in copies:
        arrived(name)
        copies[name].wait_send()


def local(hyena_q, hyena_k, hyena_v, filters, direct, queries, keys, values, segment_ids, out_weight):
    rows, feat = queries.shape
    chans = hyena_k.shape[1]
    heads = feat // HD
    groups = filters.shape[0]
    depth = out_weight.shape[0]
    bf16, f32, i32 = jnp.bfloat16, jnp.float32, jnp.int32
    dma = pltpu.SemaphoreType.DMA
    vmem = pltpu.VMEM
    scratch = [
        vmem((rows, chans), bf16), vmem((rows, chans), bf16), vmem((rows, chans), bf16),
        vmem((groups, TAPS), bf16), vmem((1, chans), bf16),
        vmem((heads, rows, HD), bf16), vmem((heads, rows, HD), bf16), vmem((heads, rows, HD), bf16),
        vmem((heads, HD, rows), bf16), vmem((1, rows), i32), vmem((depth, chans), bf16),
        vmem((QUERY_HOPS, heads, rows, HD), bf16), vmem((QUERY_HOPS, 1, rows), i32),
        vmem((KEY_HOPS, heads, rows, HD), bf16), vmem((KEY_HOPS, heads, HD, rows), bf16), vmem((KEY_HOPS, 1, rows), i32),
        vmem((KEY_HOPS + 1, rows, HD), f32), vmem((TAPS + rows, chans), bf16), vmem((groups, 2 * TAPS), f32),
        vmem((QUERY_HOPS, heads, HD, rows), f32), vmem((QUERY_HOPS, heads, 2, rows), f32),
        vmem((QUERY_HOPS, heads, HD, rows), bf16), vmem((QUERY_HOPS, heads, 2, rows), f32),
        vmem((QUERY_HOPS, heads, HD, rows), bf16), vmem((QUERY_HOPS, heads, 2, rows), f32),
        vmem((heads, HD, rows), f32), vmem((heads, 2, rows), f32),
        vmem((heads // 2, rows, 2 * HD), bf16), vmem((3, heads // 2, rows, 2 * HD), bf16), vmem((rows, chans), f32),
        dma((7,)), dma((3, heads)), dma((2, QUERY_HOPS, heads)), dma((2, KEY_HOPS, heads)), dma((2, KEY_HOPS, heads)),
        dma((2, QUERY_HOPS)), dma((2, KEY_HOPS)), dma((2, heads)), dma((2, QUERY_HOPS, heads)), dma((2, QUERY_HOPS, heads)),
        dma((2, 3, heads)),
    ]
    return pl.pallas_call(
        functools.partial(kernel, heads, plan(heads, chans // 128)),
        out_shape=(jax.ShapeDtypeStruct((rows, chans), bf16), jax.ShapeDtypeStruct((rows, chans), bf16)),
        in_specs=[pl.BlockSpec(memory_space=pl.ANY)] * 10,
        out_specs=[pl.BlockSpec(memory_space=pltpu.VMEM)] * 2,
        scratch_shapes=scratch,
        name="mixers",
        compiler_params=pltpu.CompilerParams(collective_id=0, has_side_effects=True, vmem_limit_bytes=60 << 20),
    )(
        hyena_q, hyena_k, hyena_v, filters, direct.reshape(1, chans), queries, keys, values,
        segment_ids.reshape(1, rows), out_weight,
    )


def solution(mesh):
    placed = (
        P("ctx", "tp"), P("ctx", "tp"), P("ctx", "tp"), P("tp", None), P("tp"),
        P("ctx", "tp"), P("ctx", "tp"), P("ctx", "tp"), P("ctx"), P(None, "tp"),
    )
    return jax.shard_map(
        local,
        mesh=mesh,
        in_specs=placed,
        out_specs=(P("ctx", "tp"), P("ctx", "tp")),
        check_vma=False,
    )
```

time: 212 us -> 101 us (0.48)
  the two profiles are of different devices: /device:TPU:24 before, /device:TPU:1 now
where the time goes in v1:
time: 101 us
  Pallas kernels  95 us (94%)
  local copies, waits for them, and re-layouts  5.01 us (5%)
    pallas_call x1, Pallas kernels, local(): pl.pallas_call(functools.partial(kernel, heads, plan(heads, chans // 128)...  95 us
    unnamed x2, local copies, waits for them, and re-layouts  3.74 us

profile of v1, /device:TPU:1, one launch (start us, length us, event | category | flops | bytes accessed | tf_op | source)
XLA Modules:
  0.0 100.6 jit_solution(13668472926247270282)
XLA Ops:
  0.6 1.3 %reshape.10.direct_hbm = bf16[1,1024]{1,0:T(2,128)(2,1)} reshape(bf16[1024]{0:T(1024)(128)(2,1)} %param.14) | data formatting | bytes 4096 | tf_op jit(solution)/shard_map/reshape | solution.py:427
  1.9 95.0 %mixers.1 = (bf16[256,1024]{1,0:T(8,128)(2,1)}, bf16[256,1024]{1,0:T(8,128)(2,1)}) custom-call(bf16[256,1024]{1,0:T(8,128)(2,1)} %hq_hbm.1, bf16[256,1024]{1,0:T(8,128)(2,1)} %hk_hbm.1, bf16[256,1024]{1,0:T(8,128)(2,1)} %hv_hbm.1, bf16[64,128]{1,0:T(8,128)(2,1)} %filters_hbm.1, bf16[1,1024]{1,0:T(2,128)(2,1)} %reshape.10.direct_hbm, bf16[256,512]{1,0:T(8,128)(2,1)} %q_hbm.1, ...), custom_call_target="tpu_custom_call" | custom-call | tf_op jit(solution)/shard_map/mixers/pallas_call | solution.py:418
  96.9 1.9 %copy.14 = bf16[256,1024]{1,0:T(8,128)(2,1)} copy(bf16[256,1024]{1,0:T(8,128)(2,1)} %get-tuple-element.4) | data formatting | bytes 1048576
  98.8 1.9 %copy.15 = bf16[256,1024]{1,0:T(8,128)(2,1)} copy(bf16[256,1024]{1,0:T(8,128)(2,1)} %get-tuple-element.5) | data formatting | bytes 1048576

commit v2 on v1

--- a/solution.py
+++ b/solution.py
@@ -369,7 +369,7 @@
             row = jnp.broadcast_to(taps[pl.ds(c * per + g, 1), :], (TAPS, 2 * TAPS))
             table = pltpu.roll(row, 0, 1, stride=1, stride_axis=0).astype(jnp.bfloat16)
             conv = jnp.where(group == g, jnp.dot(table, data, preferred_element_type=jnp.float32), conv)
-        gain = direct[:, lanes].astype(jnp.float32)
+        gain = direct[...].astype(jnp.float32)[c : c + 1, :]
         for b, mixed in enumerate((upper, lower)):
             span = pl.ds(b * TAPS, TAPS)
             hyena_out[span, lanes] = (
@@ -387,6 +387,23 @@
     for name in copies:
         arrived(name)
         copies[name].wait_send()
+
+
+def deliver(hyena_ref, attn_ref, hyena_out, attn_out, hyena_buf, attn_buf, sems):
+    size = hyena_buf.shape[1]
+    loads, stores = [], []
+    for i, (source, target, buf) in enumerate(((hyena_ref, hyena_out, hyena_buf), (attn_ref, attn_out, attn_buf))):
+        for j in range(2):
+            span = pl.ds(j * size, size)
+            loads.append(pltpu.make_async_copy(source.at[span, :], buf.at[j], sems.at[0, 2 * i + j]))
+            stores.append(pltpu.make_async_copy(buf.at[j], target.at[span, :], sems.at[1, 2 * i + j]))
+    for move in loads:
+        move.start()
+    for move, store in zip(loads, stores):
+        move.wait()
+        store.start()
+    for store in stores:
+        store.wait()
 
 
 def local(hyena_q, hyena_k, hyena_v, filters, direct, queries, keys, values, segment_ids, out_weight):
@@ -400,7 +417,7 @@
     vmem = pltpu.VMEM
     scratch = [
         vmem((rows, chans), bf16), vmem((rows, chans), bf16), vmem((rows, chans), bf16),
-        vmem((groups, TAPS), bf16), vmem((1, chans), bf16),
+        vmem((groups, TAPS), bf16), vmem((chans // HD, HD), bf16),
         vmem((heads, rows, HD), bf16), vmem((heads, rows, HD), bf16), vmem((heads, rows, HD), bf16),
         vmem((heads, HD, rows), bf16), vmem((1, rows), i32), vmem((depth, chans), bf16),
         vmem((QUERY_HOPS, heads, rows, HD), bf16), vmem((QUERY_HOPS, 1, rows), i32),
@@ -415,7 +432,7 @@
         dma((2, QUERY_HOPS)), dma((2, KEY_HOPS)), dma((2, heads)), dma((2, QUERY_HOPS, heads)), dma((2, QUERY_HOPS, heads)),
         dma((2, 3, heads)),
     ]
-    return pl.pallas_call(
+    hyena_out, attn_out = pl.pallas_call(
         functools.partial(kernel, heads, plan(heads, chans // 128)),
         out_shape=(jax.ShapeDtypeStruct((rows, chans), bf16), jax.ShapeDtypeStruct((rows, chans), bf16)),
         in_specs=[pl.BlockSpec(memory_space=pl.ANY)] * 10,
@@ -424,9 +441,19 @@
         name="mixers",
         compiler_params=pltpu.CompilerParams(collective_id=0, has_side_effects=True, vmem_limit_bytes=60 << 20),
     )(
-        hyena_q, hyena_k, hyena_v, filters, direct.reshape(1, chans), queries, keys, values,
+        hyena_q, hyena_k, hyena_v, filters, direct.reshape(chans // HD, HD), queries, keys, values,
         segment_ids.reshape(1, rows), out_weight,
     )
+    half = vmem((2, rows // 2, chans), bf16)
+    return pl.pallas_call(
+        deliver,
+        out_shape=(jax.ShapeDtypeStruct((rows, chans), bf16), jax.ShapeDtypeStruct((rows, chans), bf16)),
+        in_specs=[pl.BlockSpec(memory_space=pl.ANY)] * 2,
+        out_specs=[pl.BlockSpec(memory_space=pl.ANY)] * 2,
+        scratch_shapes=[half, half, dma((2, 4))],
+        name="deliver",
+        compiler_params=pltpu.CompilerParams(vmem_limit_bytes=60 << 20),
+    )(hyena_out, attn_out)
 
 
 def solution(mesh):

time: 101 us -> 97.8 us (0.968)
  local copies, waits for them, and re-layouts: 5.01 us -> 0 us
  Pallas kernels: 95 us -> 97 us
    unnamed x2 -> x0, local copies, waits for them, and re-layouts: 3.74 us -> none
    pallas_call x0 -> x1, Pallas kernels: none -> 1.98 us  [local(): pl.pallas_call(deliver, out_shape=(jax.ShapeDtypeStruct((rows, chans), bf...]
    reshape x1 -> x0, local copies, waits for them, and re-layouts: 1.28 us -> none  [local(): direct.reshape(1, chans)]
where the time goes in v2:
time: 97.8 us; the launch traced here: 97.6 us
  Pallas kernels  97 us (99%)
    pallas_call x1, Pallas kernels, local(): pl.pallas_call(functools.partial(kernel, heads, plan(heads, chans // 128)...  95 us
    pallas_call x1, Pallas kernels, local(): pl.pallas_call(deliver, out_shape=(jax.ShapeDtypeStruct((rows, chans), bf...  1.98 us

profile of v2, /device:TPU:1, one launch (start us, length us, event | category | flops | bytes accessed | tf_op | source)
XLA Modules:
  0.0 97.6 jit_solution(18200804474852781871)
XLA Ops:
  0.6 95.0 %mixers.1 = (bf16[256,1024]{1,0:T(8,128)(2,1)}, bf16[256,1024]{1,0:T(8,128)(2,1)}) custom-call(bf16[256,1024]{1,0:T(8,128)(2,1)} %hq_hbm.1, bf16[256,1024]{1,0:T(8,128)(2,1)} %hk_hbm.1, bf16[256,1024]{1,0:T(8,128)(2,1)} %hv_hbm.1, bf16[64,128]{1,0:T(8,128)(2,1)} %filters_hbm.1, bf16[8,128]{1,0:T(8,128)(2,1)} %bitcast.2, bf16[256,512]{1,0:T(8,128)(2,1)} %q_hbm.1, ...), custom_call_target="tpu_custom_call" | custom-call | tf_op jit(solution)/shard_map/mixers/pallas_call | solution.py:435
  95.6 2.0 %deliver.1 = (bf16[256,1024]{1,0:T(8,128)(2,1)}, bf16[256,1024]{1,0:T(8,128)(2,1)}) custom-call(bf16[256,1024]{1,0:T(8,128)(2,1)} %get-tuple-element.4.hyena_ref, bf16[256,1024]{1,0:T(8,128)(2,1)} %get-tuple-element.5.attn_ref), custom_call_target="tpu_custom_call" | custom-call | tf_op jit(solution)/shard_map/deliver/pallas_call | solution.py:448

commit v3 on v2

--- a/solution.py
+++ b/solution.py
@@ -15,79 +15,93 @@
 KEY_HOPS = 2
 QUERY_HOPS = WINDOW - 1 - KEY_HOPS
 NEG = -1e30
+PARTS = 2
+WEIGHTS = dict(qh=0.5, qr=-2.515, kh=0.614, kr=-2.285, k0=1.574, v0=-0.472, halo=14.128, o0=13.001, oh=5, oa=-0.97, ph=-3.06, pa=1, loc=150.0, mix=-11.49, hy=500.0, lq=1.187, lp=0.13, thr=99)
 MESH = pl.DeviceIdType.MESH
 
 
 def plan(heads, blocks):
     chunk, lag = 1.41, 1.9
-    free = {"neg": 0.0, "pos": 0.0, "tp": 0.0, "mate": 0.0}
-    ready = {}
-    order = []
-    todo = []
-
-    def add(name, needs, cost, link=None, size=1.0, rank=0):
-        todo.append(dict(name=name, needs=needs, cost=cost, link=link, size=size, rank=rank))
-
-    for r in range(1, QUERY_HOPS + 1):
-        for h in range(heads):
-            add(("q", h, r), [("q", h, r - 1)] if r > 1 else [], 0.03, "neg", 1.0, r)
-    for r in range(1, KEY_HOPS + 1):
-        for h in range(heads):
-            add(("k", h, r), [("k", h, r - 1)] if r > 1 else [], 0.03, "pos", 1.0, r)
-        for h in range(heads):
-            add(("v", h, r), [("v", h, r - 1)] if r > 1 else [("vt", h)], 0.03, "pos", 1.0, r)
+    w = WEIGHTS
+    size = 1.0 / PARTS
+    steps = {}
+
+    def add(name, needs, cost, link=None, amount=1.0, rank=0.0):
+        steps[name] = (needs, cost, link, amount, rank)
+
     for h in range(heads):
-        add(("vt", h), [], 0.15, rank=1)
-        add(("halo", h), [("mix",), ("sent", "v", heads - 1, KEY_HOPS)], 0.03, "pos", 1.0, 5)
-    add(("mix",), [], 1.0, rank=2)
+        for r in range(1, KEY_HOPS + 1):
+            turn = w["kh"] * h + w["kr"] * r
+            add(("k", h, r), [("k", h, r - 1)] if r > 1 else [], 0.03, "pos", 1.0, turn + w["k0"])
+            add(("v", h, r), [("v", h, r - 1)] if r > 1 else [("vt", h)], 0.03, "pos", 1.0, turn + w["v0"])
+        add(("vt", h), [], 0.15, rank=h - 100)
+        add(("halo", h), [("mix",)], 0.03, "pos", 1.0, w["halo"])
+        for v in range(h * PARTS, (h + 1) * PARTS):
+            at = v / PARTS
+            for r in range(1, QUERY_HOPS + 1):
+                add(("q", v, r), [("q", v, r - 1)] if r > 1 else [], 0.03, "neg", size, w["qh"] * at + w["qr"] * r)
+            for a in range(QUERY_HOPS, 0, -1):
+                needs = [("q", v, a), ("q", 0, a), ("vt", h), ("k", h, KEY_HOPS), ("v", h, KEY_HOPS), ("segk", KEY_HOPS)]
+                add(("part", v, a), needs, 0.05 + 0.35 * size, rank=100 + w["ph"] * at - w["pa"] * a)
+                needs = [("part", v, a)] + ([("o", v, a + 1)] if a < QUERY_HOPS else [])
+                cost = 0.07 + 0.13 * size if a < QUERY_HOPS else 0.05
+                add(("o", v, a), needs, cost, "pos", size, w["o0"] + w["oh"] * at - w["oa"] * a)
+            for d in range(KEY_HOPS + 1):
+                needs = [("k", h, d), ("v", h, d)] if d else [("vt", h)]
+                needs = needs + [("segk", d)] + ([("local", v, d - 1)] if d else [])
+                add(("local", v, d), needs, 0.05 + 0.35 * size, rank=w["loc"] + at)
+            add(("home", v), [("o", v, 1), ("local", v, KEY_HOPS)], 0.1 + 0.2 * size, rank=-50)
+            add(("g0", v), [("home", v)], 0.03, "mate", 0.1 * size, -40)
+            add(("g1", v), [("home", v)], 0.03, "tp", size, -45)
+            add(("g2", v), [("g1", v)], 0.03, "mate", 0.1 * size, -45)
     for d in range(KEY_HOPS + 1):
-        add(("segk", d), [("q", 0, 1)] if d == 0 else [("k", 0, d)], 0.1, rank=3)
-    for h in range(heads):
-        for a in range(QUERY_HOPS, 0, -1):
-            add(("part", h, a), [("q", h, a), ("k", h, KEY_HOPS), ("v", h, KEY_HOPS), ("segk", KEY_HOPS)], 0.4, rank=10 + (0 if a == QUERY_HOPS else 1))
-        for d in range(KEY_HOPS + 1):
-            need = [("k", h, d), ("v", h, d)] if d else [("vt", h)]
-            add(("local", h, d), need + [("segk", d)] + ([("local", h, d - 1)] if d else []), 0.4, rank=20 + d)
-        for a in range(QUERY_HOPS, 0, -1):
-            need = [("part", h, a)] + ([("o", h, a + 1)] if a < QUERY_HOPS else [])
-            add(("o", h, a), need, 0.2 if a < QUERY_HOPS else 0.05, "pos", 1.0, 4)
-        add(("home", h), [("o", h, 1), ("local", h, KEY_HOPS)], 0.3, rank=5)
-        add(("g0", h), [("home", h)], 0.03, "mate", 0.1, 6)
-        add(("g1", h), [("home", h)], 0.03, "tp", 1.0, 5)
-        add(("g2", h), [("g1", h)], 0.03, "mate", 0.1, 5)
+        add(("segk", d), [("k", 0, d)] if d else [], 0.1, rank=90)
+    add(("mix",), [], 1.0, rank=w["mix"])
     for p in range(heads // 2):
         for j, kind in enumerate(("home", "g0", "g1", "g2")):
-            add(("proj", p, j), [(kind, 2 * p), (kind, 2 * p + 1)], 0.4, rank=30 + p * 4 + j)
-    add(("taps",), [], 0.5, rank=40)
+            needs = [(kind, v) for v in range(2 * p * PARTS, 2 * (p + 1) * PARTS)]
+            add(("proj", p, j), needs, 0.4, rank=300 + 4 * p + j)
+    add(("taps",), [], 0.5, rank=400)
     for c in range(blocks):
-        add(("hyena", c), [("taps",), ("mix",)] + [("halo", h) for h in range(heads)], 1.2, rank=50)
-
-    now = 0.0
-    while todo:
-        best = None
-        horizon = None
-        for item in todo:
-            when = 0.0
-            for need in item["needs"]:
-                when = max(when, ready.get(need, math.inf))
-            if when <= now:
-                if best is None or item["rank"] < best["rank"]:
-                    best = item
-            elif when < math.inf:
-                horizon = when if horizon is None else min(horizon, when)
+        add(("hyena", c), [("taps",), ("mix",)] + [("halo", h) for h in range(heads)], 1.2, rank=w["hy"])
+
+    users = {name: [] for name in steps}
+    missing, when = {}, {}
+    for name, (needs, *_) in steps.items():
+        missing[name], when[name] = len(needs), 0.0
+        for need in needs:
+            users[need].append(name)
+    free = dict(neg=0.0, pos=0.0, tp=0.0, mate=0.0)
+    lags = dict(neg=lag + w["lq"], pos=lag + w["lp"], tp=lag, mate=0.95)
+    waiting = [name for name in steps if not missing[name]]
+    order, now = [], 0.0
+    while waiting:
+        best, best_key, later = None, None, math.inf
+        for name in waiting:
+            _, _, link, _, rank = steps[name]
+            begin = max(when[name], free[link] - w["thr"]) if link else when[name]
+            if begin <= now + 1e-9:
+                key = (0 if link or name[0] in ("vt", "home") else 1, rank)
+                if best is None or key < best_key:
+                    best, best_key = name, key
+            else:
+                later = min(later, begin)
         if best is None:
-            now = horizon
+            now = later
             continue
-        todo.remove(best)
-        order.append(best["name"])
-        now += best["cost"]
-        if best["link"]:
-            begin = max(now, free[best["link"]])
-            free[best["link"]] = begin + best["size"] * chunk
-            ready[best["name"]] = free[best["link"]] + lag
-            ready[("sent",) + best["name"]] = now
-        else:
-            ready[best["name"]] = now
+        waiting.remove(best)
+        order.append(best)
+        _, cost, link, amount, _ = steps[best]
+        now += cost
+        done = now
+        if link:
+            free[link] = max(now, free[link]) + amount * chunk
+            done = free[link] + lags[link]
+        for user in users[best]:
+            missing[user] -= 1
+            when[user] = max(when[user], done)
+            if not missing[user]:
+                waiting.append(user)
     return order
 
 
@@ -118,6 +132,10 @@
     diagonal = lax.rem(mate + 2, 4)
     rows, chans = hk.shape
     scale = math.log2(math.e) / math.sqrt(HD)
+    piece = rows // PARTS
+
+    def span_of(v):
+        return pl.ds(v % PARTS * piece, piece)
 
     loads = {}
 
@@ -162,10 +180,12 @@
         )
 
     for r in range(1, QUERY_HOPS + 1):
-        for h in range(heads):
-            copy(("q", h, r), q_own.at[h] if r == 1 else q_in.at[r - 2, h], q_in.at[r - 1, h], q_sem, (r - 1, h), {"ctx": left})
-            copy(("o", h, r), out_sum.at[r - 1, h], in_sum.at[r - 1, h], o_sem, (r - 1, h), {"ctx": right})
-            copy(("ostat", h, r), out_stat.at[r - 1, h], in_stat.at[r - 1, h], ostat_sem, (r - 1, h), {"ctx": right})
+        for v in range(heads * PARTS):
+            source = q_own.at[v // PARTS] if r == 1 else q_in.at[r - 2, v // PARTS]
+            target = q_in.at[r - 1, v // PARTS]
+            copy(("q", v, r), source.at[span_of(v), :], target.at[span_of(v), :], q_sem, (r - 1, v), {"ctx": left})
+            copy(("o", v, r), out_sum.at[r - 1, v], in_sum.at[r - 1, v], o_sem, (r - 1, v), {"ctx": right})
+            copy(("ostat", v, r), out_stat.at[r - 1, v], in_stat.at[r - 1, v], ostat_sem, (r - 1, v), {"ctx": right})
         copy(("segq", r), seg_own if r == 1 else segq_in.at[r - 2], segq_in.at[r - 1], segq_sem, (r - 1,), {"ctx": left})
     for r in range(1, KEY_HOPS + 1):
         for h in range(heads):
@@ -176,11 +196,12 @@
     for h in range(heads):
         lanes = pl.ds(h * strip, strip)
         copy(("halo", h), ext.at[pl.ds(rows, TAPS), lanes], ext.at[pl.ds(0, TAPS), lanes], halo_sem, (h,), {"ctx": right})
-        half = pl.ds(h % 2 * HD, HD)
-        mine = attn.at[h // 2, :, half]
-        copy(("g0", h), mine, attn_in.at[0, h // 2, :, half], g_sem, (0, h), {"tp": mate})
-        copy(("g1", h), mine, attn_in.at[1, h // 2, :, half], g_sem, (1, h), {"tp": across})
-        copy(("g2", h), attn_in.at[1, h // 2, :, half], attn_in.at[2, h // 2, :, half], g_sem, (2, h), {"tp": mate})
+    for v in range(heads * PARTS):
+        h = v // PARTS
+        spot = (h // 2, span_of(v), pl.ds(h % 2 * HD, HD))
+        copy(("g0", v), attn.at[spot], attn_in.at[(0,) + spot], g_sem, (0, v), {"tp": mate})
+        copy(("g1", v), attn.at[spot], attn_in.at[(1,) + spot], g_sem, (1, v), {"tp": across})
+        copy(("g2", v), attn_in.at[(1,) + spot], attn_in.at[(2,) + spot], g_sem, (2, v), {"tp": mate})
 
     got = set()
 
@@ -195,13 +216,16 @@
     def column(row):
         return jnp.transpose(jnp.broadcast_to(row.astype(jnp.float32), (HD, rows)))
 
-    def partial(query, query_seg, key, value_t, key_col, causal):
-        score = lax.dot_general(key[...], query[...], (((1,), (1,)), ((), ())), preferred_element_type=jnp.float32)
-        col = key_col[...]
-        allowed = jnp.concatenate([col] * (rows // HD), axis=1) == query_seg[...].astype(jnp.float32)
+    def partial(query, query_seg, v, key, value_t, key_col, causal):
+        score = lax.dot_general(
+            key[...], query[span_of(v), :], (((1,), (1,)), ((), ())), preferred_element_type=jnp.float32
+        )
+        col = key_col[:, :piece] if piece <= HD else jnp.concatenate([key_col[...]] * (piece // HD), axis=1)
+        allowed = col == query_seg[:, span_of(v)].astype(jnp.float32)
         if causal:
             allowed = allowed & (
-                lax.broadcasted_iota(jnp.int32, (rows, rows), 0) <= lax.broadcasted_iota(jnp.int32, (rows, rows), 1)
+                lax.broadcasted_iota(jnp.int32, (rows, piece), 0)
+                <= lax.broadcasted_iota(jnp.int32, (rows, piece), 1) + v % PARTS * piece
             )
         score = jnp.where(allowed, score * scale, NEG)
         high = jnp.max(score, axis=0, keepdims=True)
@@ -218,18 +242,18 @@
     def fetch(stat_ref, sum_ref):
         return stat_ref[0:1, :], stat_ref[1:2, :], sum_ref[...].astype(jnp.float32)
 
-    def step_q(h, r):
+    def step_q(v, r):
         if r == 1:
-            loaded(("q", h))
-            if h == 0:
+            loaded(("q", v // PARTS))
+            if v == 0:
                 loaded("seg")
         else:
-            arrived(("q", h, r - 1))
-            if h == 0:
+            arrived(("q", v, r - 1))
+            if v == 0:
                 arrived(("segq", r - 1))
-        if h == 0:
+        if v == 0:
             send(("segq", r))
-        send(("q", h, r))
+        send(("q", v, r))
 
     def step_k(h, r):
         if r == 1:
@@ -272,42 +296,46 @@
             arrived(("segk", d))
             segk_col[d] = column(segk_in[d - 1])
 
-    def step_part(h, a):
-        arrived(("q", h, a))
+    def step_part(v, a):
+        h = v // PARTS
+        arrived(("q", v, a))
         arrived(("segq", a))
         arrived(("k", h, KEY_HOPS))
         arrived(("v", h, KEY_HOPS))
-        state = partial(q_in.at[a - 1, h], segq_in.at[a - 1], k_in.at[KEY_HOPS - 1, h], vt_in.at[KEY_HOPS - 1, h], segk_col.at[KEY_HOPS], False)
+        last = KEY_HOPS - 1
+        state = partial(q_in.at[a - 1, h], segq_in.at[a - 1], v, k_in.at[last, h], vt_in.at[last, h], segk_col.at[KEY_HOPS], False)
         if a == QUERY_HOPS:
-            keep(state, out_stat.at[a - 1, h], out_sum.at[a - 1, h])
+            keep(state, out_stat.at[a - 1, v], out_sum.at[a - 1, v])
         else:
-            keep(state, part_stat.at[a - 1, h], part_sum.at[a - 1, h])
-
-    def step_local(h, d):
+            keep(state, part_stat.at[a - 1, v], part_sum.at[a - 1, v])
+
+    def step_local(v, d):
+        h = v // PARTS
         if d == 0:
-            state = partial(q_own.at[h], seg_own, k_own.at[h], vt_own.at[h], segk_col.at[0], True)
+            state = partial(q_own.at[h], seg_own, v, k_own.at[h], vt_own.at[h], segk_col.at[0], True)
         else:
             arrived(("k", h, d))
             arrived(("v", h, d))
-            state = partial(q_own.at[h], seg_own, k_in.at[d - 1, h], vt_in.at[d - 1, h], segk_col.at[d], False)
-            state = merge(fetch(local_stat.at[h], local_sum.at[h]), state)
-        keep(state, local_stat.at[h], local_sum.at[h])
-
-    def step_o(h, a):
+            state = partial(q_own.at[h], seg_own, v, k_in.at[d - 1, h], vt_in.at[d - 1, h], segk_col.at[d], False)
+            state = merge(fetch(local_stat.at[v], local_sum.at[v]), state)
+        keep(state, local_stat.at[v], local_sum.at[v])
+
+    def step_o(v, a):
         if a < QUERY_HOPS:
-            arrived(("o", h, a + 1))
-            arrived(("ostat", h, a + 1))
-            state = merge(fetch(part_stat.at[a - 1, h], part_sum.at[a - 1, h]), fetch(in_stat.at[a, h], in_sum.at[a, h]))
-            keep(state, out_stat.at[a - 1, h], out_sum.at[a - 1, h])
-        send(("o", h, a))
-        send(("ostat", h, a))
-
-    def step_home(h):
-        arrived(("o", h, 1))
-        arrived(("ostat", h, 1))
-        _, amount, summed = merge(fetch(local_stat.at[h], local_sum.at[h]), fetch(in_stat.at[0, h], in_sum.at[0, h]))
+            arrived(("ostat", v, a + 1))
+            arrived(("o", v, a + 1))
+            state = merge(fetch(part_stat.at[a - 1, v], part_sum.at[a - 1, v]), fetch(in_stat.at[a, v], in_sum.at[a, v]))
+            keep(state, out_stat.at[a - 1, v], out_sum.at[a - 1, v])
+        send(("ostat", v, a))
+        send(("o", v, a))
+
+    def step_home(v):
+        h = v // PARTS
+        arrived(("ostat", v, 1))
+        arrived(("o", v, 1))
+        _, amount, summed = merge(fetch(local_stat.at[v], local_sum.at[v]), fetch(in_stat.at[0, v], in_sum.at[0, v]))
         result = jnp.transpose(summed / amount)
-        attn[h // 2, :, pl.ds(h % 2 * HD, HD)] = result.astype(jnp.bfloat16)
+        attn[h // 2, span_of(v), pl.ds(h % 2 * HD, HD)] = result.astype(jnp.bfloat16)
 
     def step_g0(h):
         send(("g0", h))
@@ -325,7 +353,7 @@
     def step_proj(p, j):
         loaded("weight")
         if j:
-            for h in (2 * p, 2 * p + 1):
+            for h in range(2 * p * PARTS, 2 * (p + 1) * PARTS):
                 arrived((("g0", "g1", "g2")[j - 1], h))
         block = attn[p] if j == 0 else attn_in[j - 1, p]
         owner = (tp, mate, across, diagonal)[j]
@@ -412,6 +440,7 @@
     heads = feat // HD
     groups = filters.shape[0]
     depth = out_weight.shape[0]
+    pieces, piece = heads * PARTS, rows // PARTS
     bf16, f32, i32 = jnp.bfloat16, jnp.float32, jnp.int32
     dma = pltpu.SemaphoreType.DMA
     vmem = pltpu.VMEM
@@ -423,14 +452,14 @@
         vmem((QUERY_HOPS, heads, rows, HD), bf16), vmem((QUERY_HOPS, 1, rows), i32),
         vmem((KEY_HOPS, heads, rows, HD), bf16), vmem((KEY_HOPS, heads, HD, rows), bf16), vmem((KEY_HOPS, 1, rows), i32),
         vmem((KEY_HOPS + 1, rows, HD), f32), vmem((TAPS + rows, chans), bf16), vmem((groups, 2 * TAPS), f32),
-        vmem((QUERY_HOPS, heads, HD, rows), f32), vmem((QUERY_HOPS, heads, 2, rows), f32),
-        vmem((QUERY_HOPS, heads, HD, rows), bf16), vmem((QUERY_HOPS, heads, 2, rows), f32),
-        vmem((QUERY_HOPS, heads, HD, rows), bf16), vmem((QUERY_HOPS, heads, 2, rows), f32),
-        vmem((heads, HD, rows), f32), vmem((heads, 2, rows), f32),
+        vmem((QUERY_HOPS, pieces, HD, piece), f32), vmem((QUERY_HOPS, pieces, 2, piece), f32),
+        vmem((QUERY_HOPS, pieces, HD, piece), bf16), vmem((QUERY_HOPS, pieces, 2, piece), f32),
+        vmem((QUERY_HOPS, pieces, HD, piece), bf16), vmem((QUERY_HOPS, pieces, 2, piece), f32),
+        vmem((pieces, HD, piece), f32), vmem((pieces, 2, piece), f32),
         vmem((heads // 2, rows, 2 * HD), bf16), vmem((3, heads // 2, rows, 2 * HD), bf16), vmem((rows, chans), f32),
-        dma((7,)), dma((3, heads)), dma((2, QUERY_HOPS, heads)), dma((2, KEY_HOPS, heads)), dma((2, KEY_HOPS, heads)),
-        dma((2, QUERY_HOPS)), dma((2, KEY_HOPS)), dma((2, heads)), dma((2, QUERY_HOPS, heads)), dma((2, QUERY_HOPS, heads)),
-        dma((2, 3, heads)),
+        dma((7,)), dma((3, heads)), dma((2, QUERY_HOPS, pieces)), dma((2, KEY_HOPS, heads)), dma((2, KEY_HOPS, heads)),
+        dma((2, QUERY_HOPS)), dma((2, KEY_HOPS)), dma((2, heads)), dma((2, QUERY_HOPS, pieces)), dma((2, QUERY_HOPS, pieces)),
+        dma((2, 3, pieces)),
     ]
     hyena_out, attn_out = pl.pallas_call(
         functools.partial(kernel, heads, plan(heads, chans // 128)),

time: 97.8 us -> 100 us (1.022)
  Pallas kernels: 97 us -> 99.6 us
    pallas_call x1, Pallas kernels: 95 us -> 97.6 us  [local(): pl.pallas_call(functools.partial(kernel, heads, plan(heads, chans // 128)...]
where the time goes in v3:
time: 100 us
  Pallas kernels  99.6 us (100%)
    pallas_call x1, Pallas kernels, local(): pl.pallas_call(functools.partial(kernel, heads, plan(heads, chans // 128)...  97.6 us

profile of v3, /device:TPU:1, one launch (start us, length us, event | category | flops | bytes accessed | tf_op | source)
XLA Modules:
  0.0 100.3 jit_solution(11049364209431839065)
XLA Ops:
  0.6 97.6 %mixers.1 = (bf16[256,1024]{1,0:T(8,128)(2,1)}, bf16[256,1024]{1,0:T(8,128)(2,1)}) custom-call(bf16[256,1024]{1,0:T(8,128)(2,1)} %hq_hbm.1, bf16[256,1024]{1,0:T(8,128)(2,1)} %hk_hbm.1, bf16[256,1024]{1,0:T(8,128)(2,1)} %hv_hbm.1, bf16[64,128]{1,0:T(8,128)(2,1)} %filters_hbm.1, bf16[8,128]{1,0:T(8,128)(2,1)} %bitcast.2, bf16[256,512]{1,0:T(8,128)(2,1)} %q_hbm.1, ...), custom_call_target="tpu_custom_call" | custom-call | tf_op jit(solution)/shard_map/mixers/pallas_call | solution.py:464
  98.3 2.0 %deliver.1 = (bf16[256,1024]{1,0:T(8,128)(2,1)}, bf16[256,1024]{1,0:T(8,128)(2,1)}) custom-call(bf16[256,1024]{1,0:T(8,128)(2,1)} %get-tuple-element.4.hyena_ref, bf16[256,1024]{1,0:T(8,128)(2,1)} %get-tuple-element.5.attn_ref), custom_call_target="tpu_custom_call" | custom-call | tf_op jit(solution)/shard_map/deliver/pallas_call | solution.py:477

commit v4 on v2

--- a/solution.py
+++ b/solution.py
@@ -18,77 +18,26 @@
 MESH = pl.DeviceIdType.MESH
 
 
-def plan(heads, blocks):
-    chunk, lag = 1.41, 1.9
-    free = {"neg": 0.0, "pos": 0.0, "tp": 0.0, "mate": 0.0}
-    ready = {}
-    order = []
-    todo = []
-
-    def add(name, needs, cost, link=None, size=1.0, rank=0):
-        todo.append(dict(name=name, needs=needs, cost=cost, link=link, size=size, rank=rank))
-
-    for r in range(1, QUERY_HOPS + 1):
-        for h in range(heads):
-            add(("q", h, r), [("q", h, r - 1)] if r > 1 else [], 0.03, "neg", 1.0, r)
-    for r in range(1, KEY_HOPS + 1):
-        for h in range(heads):
-            add(("k", h, r), [("k", h, r - 1)] if r > 1 else [], 0.03, "pos", 1.0, r)
-        for h in range(heads):
-            add(("v", h, r), [("v", h, r - 1)] if r > 1 else [("vt", h)], 0.03, "pos", 1.0, r)
-    for h in range(heads):
-        add(("vt", h), [], 0.15, rank=1)
-        add(("halo", h), [("mix",), ("sent", "v", heads - 1, KEY_HOPS)], 0.03, "pos", 1.0, 5)
-    add(("mix",), [], 1.0, rank=2)
-    for d in range(KEY_HOPS + 1):
-        add(("segk", d), [("q", 0, 1)] if d == 0 else [("k", 0, d)], 0.1, rank=3)
-    for h in range(heads):
-        for a in range(QUERY_HOPS, 0, -1):
-            add(("part", h, a), [("q", h, a), ("k", h, KEY_HOPS), ("v", h, KEY_HOPS), ("segk", KEY_HOPS)], 0.4, rank=10 + (0 if a == QUERY_HOPS else 1))
-        for d in range(KEY_HOPS + 1):
-            need = [("k", h, d), ("v", h, d)] if d else [("vt", h)]
-            add(("local", h, d), need + [("segk", d)] + ([("local", h, d - 1)] if d else []), 0.4, rank=20 + d)
-        for a in range(QUERY_HOPS, 0, -1):
-            need = [("part", h, a)] + ([("o", h, a + 1)] if a < QUERY_HOPS else [])
-            add(("o", h, a), need, 0.2 if a < QUERY_HOPS else 0.05, "pos", 1.0, 4)
-        add(("home", h), [("o", h, 1), ("local", h, KEY_HOPS)], 0.3, rank=5)
-        add(("g0", h), [("home", h)], 0.03, "mate", 0.1, 6)
-        add(("g1", h), [("home", h)], 0.03, "tp", 1.0, 5)
-        add(("g2", h), [("g1", h)], 0.03, "mate", 0.1, 5)
-    for p in range(heads // 2):
-        for j, kind in enumerate(("home", "g0", "g1", "g2")):
-            add(("proj", p, j), [(kind, 2 * p), (kind, 2 * p + 1)], 0.4, rank=30 + p * 4 + j)
-    add(("taps",), [], 0.5, rank=40)
-    for c in range(blocks):
-        add(("hyena", c), [("taps",), ("mix",)] + [("halo", h) for h in range(heads)], 1.2, rank=50)
-
-    now = 0.0
-    while todo:
-        best = None
-        horizon = None
-        for item in todo:
-            when = 0.0
-            for need in item["needs"]:
-                when = max(when, ready.get(need, math.inf))
-            if when <= now:
-                if best is None or item["rank"] < best["rank"]:
-                    best = item
-            elif when < math.inf:
-                horizon = when if horizon is None else min(horizon, when)
-        if best is None:
-            now = horizon
-            continue
-        todo.remove(best)
-        order.append(best["name"])
-        now += best["cost"]
-        if best["link"]:
-            begin = max(now, free[best["link"]])
-            free[best["link"]] = begin + best["size"] * chunk
-            ready[best["name"]] = free[best["link"]] + lag
-            ready[("sent",) + best["name"]] = now
-        else:
-            ready[best["name"]] = now
-    return order
+ORDER = (
+    ("q", 1, 1), ("k", 2, 1), ("segk", 0), ("taps",), ("vt", 0), ("k", 0, 1), ("v", 0, 1), ("k", 3, 1), ("q", 0, 1),
+    ("vt", 3), ("k", 1, 1), ("vt", 2), ("local", 0, 0), ("q", 2, 1), ("vt", 1), ("v", 3, 1), ("v", 2, 1),
+    ("v", 1, 1), ("q", 1, 2), ("local", 2, 0), ("q", 3, 1), ("segk", 1), ("k", 2, 2), ("q", 2, 2), ("k", 0, 2),
+    ("local", 1, 0), ("q", 0, 2), ("v", 0, 2), ("q", 3, 2), ("mix",), ("k", 1, 2), ("q", 2, 3), ("q", 0, 3),
+    ("q", 1, 3), ("local", 0, 1), ("v", 3, 2), ("q", 3, 3), ("local", 2, 1), ("halo", 0), ("halo", 2), ("q", 0, 4),
+    ("v", 1, 2), ("halo", 3), ("q", 1, 4), ("q", 2, 4), ("q", 0, 5), ("halo", 1), ("q", 1, 5), ("segk", 2),
+    ("k", 3, 2), ("v", 2, 2), ("part", 0, 1), ("part", 0, 2), ("local", 1, 1), ("q", 3, 4), ("q", 2, 5),
+    ("part", 0, 4), ("part", 0, 5), ("o", 0, 5), ("part", 0, 3), ("part", 1, 1), ("part", 1, 5), ("o", 1, 5),
+    ("q", 3, 5), ("o", 0, 4), ("part", 1, 4), ("part", 3, 4), ("local", 1, 2), ("o", 1, 4), ("part", 2, 5),
+    ("o", 2, 5), ("hyena", 0), ("part", 3, 3), ("part", 3, 5), ("o", 3, 5), ("hyena", 5), ("part", 1, 2),
+    ("o", 0, 3), ("part", 1, 3), ("o", 1, 3), ("part", 3, 1), ("part", 2, 1), ("part", 2, 4), ("o", 2, 4),
+    ("o", 3, 4), ("part", 2, 3), ("hyena", 2), ("o", 0, 2), ("o", 1, 2), ("local", 0, 2), ("part", 3, 2),
+    ("hyena", 3), ("o", 2, 3), ("hyena", 1), ("o", 3, 3), ("o", 0, 1), ("hyena", 7), ("o", 1, 1), ("part", 2, 2),
+    ("o", 2, 2), ("o", 3, 2), ("local", 3, 0), ("local", 3, 1), ("home", 0), ("g1", 0), ("local", 2, 2),
+    ("local", 3, 2), ("hyena", 4), ("g0", 0), ("home", 1), ("o", 2, 1), ("g1", 1), ("g0", 1), ("hyena", 6),
+    ("o", 3, 1), ("home", 2), ("g1", 2), ("home", 3), ("g1", 3), ("g0", 3), ("g2", 1), ("g2", 0), ("proj", 1, 0),
+    ("proj", 0, 0), ("g0", 2), ("proj", 0, 3), ("g2", 2), ("proj", 1, 1), ("proj", 0, 2), ("proj", 0, 1), ("g2", 3),
+    ("proj", 1, 2), ("proj", 1, 3),
+)
 
 
 def merge(first, second):
@@ -103,12 +52,12 @@
     heads,
     order,
     hq_hbm, hk_hbm, hv_hbm, filters_hbm, direct_hbm, q_hbm, k_hbm, v_hbm, seg_hbm, w_hbm,
-    hyena_out, attn_out,
-    hq, hk, hv, filters, direct, q_own, k_own, v_own, vt_own, seg_own, weight,
+    hyena_hbm, attn_hbm,
+    hyena_out, attn_out, hq, hk, hv, filters, direct, q_own, k_own, v_own, vt_own, seg_own, weight,
     q_in, segq_in, k_in, vt_in, segk_in, segk_col, ext, taps,
     part_sum, part_stat, out_sum, out_stat, in_sum, in_stat, local_sum, local_stat,
     attn, attn_in, total,
-    load_sem, head_sem, q_sem, k_sem, v_sem, segq_sem, segk_sem, halo_sem, o_sem, ostat_sem, g_sem,
+    load_sem, head_sem, q_sem, k_sem, v_sem, segq_sem, segk_sem, halo_sem, o_sem, ostat_sem, g_sem, out_sem,
 ):
     ctx, tp = lax.axis_index("ctx"), lax.axis_index("tp")
     count = lax.axis_size("ctx")
@@ -138,6 +87,11 @@
     load("weight", w_hbm, weight, load_sem.at[6])
 
     done = set()
+    stores = []
+
+    def store(source, target, lanes, sem):
+        stores.append(pltpu.make_async_copy(source.at[:, lanes], target.at[:, lanes], sem))
+        stores[-1].start()
 
     def loaded(name):
         if name not in done:
@@ -339,6 +293,7 @@
                 term = total[:, lanes] + term
             if last:
                 attn_out[:, lanes] = term.astype(jnp.bfloat16)
+                store(attn_out, attn_hbm, lanes, out_sem.at[1, lo // width])
             else:
                 total[:, lanes] = term
 
@@ -376,6 +331,7 @@
                 hq[span, lanes].astype(jnp.float32)
                 * (conv[:, b * TAPS : (b + 1) * TAPS] + gain * mixed.astype(jnp.float32))
             ).astype(jnp.bfloat16)
+        store(hyena_out, hyena_hbm, lanes, out_sem.at[0, c])
 
     steps = dict(
         q=step_q, k=step_k, vt=step_vt, v=step_v, mix=step_mix, halo=step_halo, segk=step_segk, part=step_part,
@@ -387,6 +343,8 @@
     for name in copies:
         arrived(name)
         copies[name].wait_send()
+    for move in stores:
+        move.wait()
 
 
 def deliver(hyena_ref, attn_ref, hyena_out, attn_out, hyena_buf, attn_buf, sems):
@@ -416,6 +374,7 @@
     dma = pltpu.SemaphoreType.DMA
     vmem = pltpu.VMEM
     scratch = [
+        vmem((rows, chans), bf16), vmem((rows, chans), bf16),
         vmem((rows, chans), bf16), vmem((rows, chans), bf16), vmem((rows, chans), bf16),
         vmem((groups, TAPS), bf16), vmem((chans // HD, HD), bf16),
         vmem((heads, rows, HD), bf16), vmem((heads, rows, HD), bf16), vmem((heads, rows, HD), bf16),
@@ -430,13 +389,13 @@
         vmem((heads // 2, rows, 2 * HD), bf16), vmem((3, heads // 2, rows, 2 * HD), bf16), vmem((rows, chans), f32),
         dma((7,)), dma((3, heads)), dma((2, QUERY_HOPS, heads)), dma((2, KEY_HOPS, heads)), dma((2, KEY_HOPS, heads)),
         dma((2, QUERY_HOPS)), dma((2, KEY_HOPS)), dma((2, heads)), dma((2, QUERY_HOPS, heads)), dma((2, QUERY_HOPS, heads)),
-        dma((2, 3, heads)),
+        dma((2, 3, heads)), dma((2, chans // HD)),
     ]
     hyena_out, attn_out = pl.pallas_call(
-        functools.partial(kernel, heads, plan(heads, chans // 128)),
+        functools.partial(kernel, heads, ORDER),
         out_shape=(jax.ShapeDtypeStruct((rows, chans), bf16), jax.ShapeDtypeStruct((rows, chans), bf16)),
         in_specs=[pl.BlockSpec(memory_space=pl.ANY)] * 10,
-        out_specs=[pl.BlockSpec(memory_space=pltpu.VMEM)] * 2,
+        out_specs=[pl.BlockSpec(memory_space=pl.ANY)] * 2,
         scratch_shapes=scratch,
         name="mixers",
         compiler_params=pltpu.CompilerParams(collective_id=0, has_side_effects=True, vmem_limit_bytes=60 << 20),

time: 97.8 us -> 95.7 us (0.979)
  Pallas kernels: 97 us -> 94.9 us
    pallas_call x1, Pallas kernels: 95 us -> 93 us  [local(): pl.pallas_call(functools.partial(kernel, heads, ORDER), out_shape=(jax.Sh...]
where the time goes in v4:
time: 95.7 us; the launch traced here: 95.6 us
  Pallas kernels  94.9 us (99%)
    pallas_call x1, Pallas kernels, local(): pl.pallas_call(functools.partial(kernel, heads, ORDER), out_shape=(jax.Sh...  93 us
    pallas_call x1, Pallas kernels, local(): pl.pallas_call(deliver, out_shape=(jax.ShapeDtypeStruct((rows, chans), bf...  1.98 us

profile of v4, /device:TPU:1, one launch (start us, length us, event | category | flops | bytes accessed | tf_op | source)
XLA Modules:
  0.0 95.6 jit_solution(12630980254107300958)
XLA Ops:
  0.6 93.0 %mixers.1 = (bf16[256,1024]{1,0:T(8,128)(2,1)}, bf16[256,1024]{1,0:T(8,128)(2,1)}) custom-call(bf16[256,1024]{1,0:T(8,128)(2,1)} %hq_hbm.1, bf16[256,1024]{1,0:T(8,128)(2,1)} %hk_hbm.1, bf16[256,1024]{1,0:T(8,128)(2,1)} %hv_hbm.1, bf16[64,128]{1,0:T(8,128)(2,1)} %filters_hbm.1, bf16[8,128]{1,0:T(8,128)(2,1)} %bitcast.2, bf16[256,512]{1,0:T(8,128)(2,1)} %q_hbm.1, ...), custom_call_target="tpu_custom_call" | custom-call | tf_op jit(solution)/shard_map/mixers/pallas_call | solution.py:394
  93.6 2.0 %deliver.1 = (bf16[256,1024]{1,0:T(8,128)(2,1)}, bf16[256,1024]{1,0:T(8,128)(2,1)}) custom-call(bf16[256,1024]{1,0:T(8,128)(2,1)} %get-tuple-element.4.hyena_ref, bf16[256,1024]{1,0:T(8,128)(2,1)} %get-tuple-element.5.attn_ref), custom_call_target="tpu_custom_call" | custom-call | tf_op jit(solution)/shard_map/deliver/pallas_call | solution.py:407

commit v5 on v4

--- a/solution.py
+++ b/solution.py
@@ -68,6 +68,10 @@
     rows, chans = hk.shape
     scale = math.log2(math.e) / math.sqrt(HD)
 
+    barrier = pltpu.get_barrier_semaphore()
+    for peer in ({"ctx": left}, {"ctx": right}, {"tp": mate}, {"tp": across}):
+        pl.semaphore_signal(barrier, inc=1, device_id=peer, device_id_type=MESH)
+
     loads = {}
 
     def load(name, source, target, sem):
@@ -98,9 +102,6 @@
             done.add(name)
             loads[name].wait()
 
-    barrier = pltpu.get_barrier_semaphore()
-    for peer in ({"ctx": left}, {"ctx": right}, {"tp": mate}, {"tp": across}):
-        pl.semaphore_signal(barrier, inc=1, device_id=peer, device_id_type=MESH)
     pl.semaphore_wait(barrier, 4)
 
     copies = {}

time: 95.7 us -> 95.6 us (level)
  no operation moved by 1% of the time
where the time goes in v5:
time: 95.6 us; the launch traced here: 95.5 us
  Pallas kernels  94.8 us (99%)
    pallas_call x1, Pallas kernels, local(): pl.pallas_call(functools.partial(kernel, heads, ORDER), out_shape=(jax.Sh...  92.8 us
    pallas_call x1, Pallas kernels, local(): pl.pallas_call(deliver, out_shape=(jax.ShapeDtypeStruct((rows, chans), bf...  1.98 us

profile of v5, /device:TPU:1, one launch (start us, length us, event | category | flops | bytes accessed | tf_op | source)
XLA Modules:
  0.0 95.5 jit_solution(7785376962660601738)
XLA Ops:
  0.6 92.8 %mixers.1 = (bf16[256,1024]{1,0:T(8,128)(2,1)}, bf16[256,1024]{1,0:T(8,128)(2,1)}) custom-call(bf16[256,1024]{1,0:T(8,128)(2,1)} %hq_hbm.1, bf16[256,1024]{1,0:T(8,128)(2,1)} %hk_hbm.1, bf16[256,1024]{1,0:T(8,128)(2,1)} %hv_hbm.1, bf16[64,128]{1,0:T(8,128)(2,1)} %filters_hbm.1, bf16[8,128]{1,0:T(8,128)(2,1)} %bitcast.2, bf16[256,512]{1,0:T(8,128)(2,1)} %q_hbm.1, ...), custom_call_target="tpu_custom_call" | custom-call | tf_op jit(solution)/shard_map/mixers/pallas_call | solution.py:395
  93.5 2.0 %deliver.1 = (bf16[256,1024]{1,0:T(8,128)(2,1)}, bf16[256,1024]{1,0:T(8,128)(2,1)}) custom-call(bf16[256,1024]{1,0:T(8,128)(2,1)} %get-tuple-element.4.hyena_ref, bf16[256,1024]{1,0:T(8,128)(2,1)} %get-tuple-element.5.attn_ref), custom_call_target="tpu_custom_call" | custom-call | tf_op jit(solution)/shard_map/deliver/pallas_call | solution.py:408
